TPU v7x, 512 devices: a whole 4x4x16 slice. The times are simulated.
512 devices in a mesh: dp: 32 (over z, core), expert: 16 (over x, y).
Axes of the slice: x: 4, y: 4, z: 16, core: 2. Of those that a mesh axis runs over, the one named last changes fastest.
Arguments:
- tokens: bfloat16 [5120, 4096], P('expert', 'dp'), may hold values from -6 to 6
- out_grad: bfloat16 [5120, 4096], P('expert', 'dp'), may hold values from -0.29882812 to 0.29882812
- slot_tokens: int32 [4, 160], replicated, may hold values from 0 to 5119, as said below
- slot_gate: float32 [4, 160], replicated, may hold values from 0.1 to 1
- w_gate: bfloat16 [16, 4096, 2048], P('expert', 'dp'), may hold values from -0.09375 to 0.09375
- w_up: bfloat16 [16, 4096, 2048], P('expert', 'dp'), may hold values from -0.09375 to 0.09375
- w_down: bfloat16 [16, 2048, 4096], P('expert', None, 'dp'), may hold values from -0.0625 to 0.0625
Outputs:
- grad_tokens: bfloat16 [5120, 4096], P('expert', 'dp')
- grad_w_gate: bfloat16 [16, 4096, 2048], P('expert', 'dp')
- grad_w_up: bfloat16 [16, 4096, 2048], P('expert', 'dp')
- grad_w_down: bfloat16 [16, 2048, 4096], P('expert', None, 'dp')
- grad_gates: float32 [16, 40], P('expert')
Inputs may be any that keep to these rules, and one draw needn't show every extreme that they name: `slot_tokens`: row e lists 160 distinct token numbers, ordered by their owner t // 320 ascending. At most 20 of a row come from the 320 tokens of one owner, and in every row exactly 20 come from one owner.
All inputs are finite; a program needn't handle non-finite values.
Results may differ from a plain program's by a relative error of at most 0.0057.
Values may be sent and summed in bfloat16 or wider, within the bound.
No kernel may reach another device: no remote copies, remote signals or barrier semaphores. Data moves between devices by JAX's collectives and lax.ppermute only.
A program may use at most 64 MiB of HBM per device.

v0:
```python
import jax
import jax.numpy as jnp
from jax import lax
from jax.sharding import PartitionSpec as P

GROUP = 4


def partner(value, axis, distance):
    mask = 2**distance
    pairs = [(source, source ^ mask) for source in range(lax.axis_size(axis))]
    return lax.ppermute(value, axis, pairs)


def contract_rows(left, right):
    return lax.dot_general(
        left, right, (((0,), (0,)), ((), ())), preferred_element_type=jnp.float32
    )


def contract_cols(left, right):
    return lax.dot_general(
        left, right, (((1,), (1,)), ((), ())), preferred_element_type=jnp.float32
    )


def slot_ranking(owners, owner_count):
    owner_range = jnp.arange(owner_count, dtype=jnp.int32)
    onehot = (owners[:, :, None] == owner_range[None, None, :]).astype(jnp.int32)
    before = jnp.cumsum(onehot, axis=1) - onehot
    return jnp.sum(before * onehot, axis=2)


def gated_grads(upstream, pre_gate, pre_up, sigmoid_gate):
    gate_side = (upstream * pre_up * sigmoid_gate * (1.0 + pre_gate * (1.0 - sigmoid_gate))).astype(
        jnp.bfloat16
    )
    up_side = (upstream * pre_gate * sigmoid_gate).astype(jnp.bfloat16)
    return (gate_side, up_side)


def per_device(tokens, out_grad, slot_tokens, slot_gate, w_gate, w_up, w_down):
    owner_count = lax.axis_size("expert")
    position = lax.axis_index("expert")
    token_rows = tokens.shape[0]
    feature_cols = tokens.shape[1]
    flight_count, capacity = slot_tokens.shape
    bucket_size = GROUP * max(1, capacity // (2 * owner_count))
    owners = slot_tokens // token_rows
    slot_rank = slot_ranking(owners, owner_count)
    is_mine = owners == position
    local_index = slot_tokens - position * token_rows
    expert_rows = jnp.broadcast_to(
        jnp.arange(flight_count, dtype=jnp.int32)[:, None], (flight_count, capacity)
    )
    column_index = jnp.where(is_mine, slot_rank, bucket_size)
    send_table = (
        jnp.zeros((flight_count, bucket_size + 1), jnp.int32)
        .at[expert_rows, column_index]
        .set(local_index)[:, :bucket_size]
    )
    filled = (
        jnp.zeros((flight_count, bucket_size + 1), jnp.int32)
        .at[expert_rows, column_index]
        .set(1)[:, :bucket_size]
    )
    send_index = jnp.repeat(send_table, GROUP, axis=0)
    send_valid = jnp.repeat(filled, GROUP, axis=0) > 0
    input_send = jnp.where(send_valid[:, :, None], tokens[send_index], jnp.zeros((), jnp.bfloat16))
    grad_send = jnp.where(send_valid[:, :, None], out_grad[send_index], jnp.zeros((), jnp.bfloat16))
    input_recv, grad_recv = (
        lax.all_to_all(input_send, "expert", split_axis=0, concat_axis=0, tiled=True),
        lax.all_to_all(grad_send, "expert", split_axis=0, concat_axis=0, tiled=True),
    )
    expert_here = position // GROUP
    quarter = position % GROUP
    owner_here = lax.dynamic_index_in_dim(owners, expert_here, 0, keepdims=False)
    rank_here = lax.dynamic_index_in_dim(slot_rank, expert_here, 0, keepdims=False)
    bucket_flat = owner_here * bucket_size + rank_here
    slot_inputs = input_recv.reshape(owner_count * bucket_size, feature_cols)[bucket_flat]
    slot_grads = grad_recv.reshape(owner_count * bucket_size, feature_cols)[bucket_flat]
    gates_here = lax.dynamic_index_in_dim(slot_gate, expert_here, 0, keepdims=False)
    gate_weight = w_gate[0]
    up_weight = w_up[0]
    down_weight = w_down[0]
    part_gate = jnp.dot(slot_inputs, gate_weight, preferred_element_type=jnp.float32)
    part_up = jnp.dot(slot_inputs, up_weight, preferred_element_type=jnp.float32)
    pre_gate, pre_up = lax.psum((part_gate, part_up), "dp")
    sigmoid_gate = jax.nn.sigmoid(pre_gate)
    hidden = (pre_gate * sigmoid_gate * pre_up).astype(jnp.bfloat16)
    local_out = jnp.dot(hidden, down_weight, preferred_element_type=jnp.float32)
    gate_part = jnp.sum(slot_grads.astype(jnp.float32) * local_out, axis=1)
    scaled = (gates_here[:, None] * slot_grads.astype(jnp.float32)).astype(jnp.bfloat16)
    grad_down = contract_rows(hidden, scaled).astype(jnp.bfloat16)
    part_hidden = contract_cols(scaled, down_weight)
    grad_hidden = lax.psum(part_hidden, "dp")
    gate_side, up_side = gated_grads(grad_hidden, pre_gate, pre_up, sigmoid_gate)
    gate_total = lax.psum(gate_part, "dp")
    grad_gate_weight = contract_rows(slot_inputs, gate_side).astype(jnp.bfloat16)
    grad_up_weight = contract_rows(slot_inputs, up_side).astype(jnp.bfloat16)
    slot_back = contract_cols(gate_side, gate_weight) + contract_cols(up_side, up_weight)
    for bit_number in range(GROUP.bit_length() - 1):
        gate_total = gate_total + partner(gate_total, "expert", bit_number)
    outgoing = (
        jnp.zeros((owner_count * bucket_size, feature_cols), jnp.float32)
        .at[bucket_flat]
        .set(slot_back)
    )
    incoming = lax.all_to_all(
        outgoing.reshape(owner_count, bucket_size, feature_cols),
        "expert",
        split_axis=0,
        concat_axis=0,
        tiled=True,
    )
    target = jnp.where(send_valid, send_index, token_rows)
    summed = (
        jnp.zeros((token_rows + 1, feature_cols), jnp.float32)
        .at[target.reshape(-1)]
        .add(incoming.reshape(-1, feature_cols))
    )
    grad_tokens = summed[:token_rows].astype(jnp.bfloat16)
    gate_width = capacity // GROUP
    grad_gates = lax.dynamic_slice_in_dim(gate_total, quarter * gate_width, gate_width)[None, :]
    return (grad_tokens, grad_gate_weight[None], grad_up_weight[None], grad_down[None], grad_gates)


def solution(mesh):
    in_specs = (
        P("expert", "dp"),
        P("expert", "dp"),
        P(),
        P(),
        P("expert", "dp", None),
        P("expert", "dp", None),
        P("expert", None, "dp"),
    )
    out_specs = (
        P("expert", "dp"),
        P("expert", "dp", None),
        P("expert", "dp", None),
        P("expert", None, "dp"),
        P("expert", None),
    )
    return jax.shard_map(
        per_device, mesh=mesh, in_specs=in_specs, out_specs=out_specs, check_vma=False
    )
```

profile of v0, /device:TPU:2, one launch (start us, length us, event | category | flops | bytes accessed | tf_op | source)
XLA Modules:
  0.0 412.5 jit_solution(8496324978233504566)
XLA Ops:
  8.1 2.3 reduce-window.6
  10.8 29.9 %scatter_fusion = s32[4,21]{1,0:T(4,128)S(1)} fusion(s32[4,21]{1,0:T(4,128)S(1)} %broadcast.144.clone.1, s32[640]{0:T(1024)S(1)} %reshape.195, s32[640]{0:T(1024)S(1)} %broadcast.189), kind=kCustom, calls=%fused_computation.4 | custom fusion | bytes 12800 | tf_op jit(solution)/shard_map/scatter | solution.py:65
  40.7 29.9 %scatter_fusion.1 = s32[4,21]{1,0:T(4,128)S(1)} fusion(s32[4,21]{1,0:T(4,128)S(1)} %broadcast.144.clone, s32[640]{0:T(1024)S(1)} %reshape.195, s32[640]{0:T(1024)S(1)} %reshape.203), kind=kCustom, calls=%fused_computation.5 | custom fusion | bytes 12800 | tf_op jit(solution)/shard_map/scatter | solution.py:60
  70.7 1.4 gather_fusion.2
  72.2 1.4 gather_fusion
  74.4 9.2 %all-to-all-start = ((bf16[16,20,128]{2,1,0:T(8,128)(2,1)}), bf16[16,20,128]{2,1,0:T(8,128)(2,1)S(1)}, u32[]{:S(2)}, u32[]{:S(2)}) async-start(bf16[16,20,128]{2,1,0:T(8,128)(2,1)} %get-tuple-element.13), calls=%async_computation | async-start | bytes 196608 | tf_op jit(solution)/shard_map/all_to_all | solution.py:73
  83.7 6.4 %all-to-all-done = bf16[16,20,128]{2,1,0:T(8,128)(2,1)S(1)} async-done(((bf16[16,20,128]{2,1,0:T(8,128)(2,1)}), bf16[16,20,128]{2,1,0:T(8,128)(2,1)S(1)}, u32[]{:S(2)}, u32[]{:S(2)}) %all-to-all-start) | async-done | bytes 81952 | tf_op jit(solution)/shard_map/all_to_all | solution.py:73
  90.0 5.0 %all-to-all-start.1 = ((bf16[16,20,128]{2,1,0:T(8,128)(2,1)}), bf16[16,20,128]{2,1,0:T(8,128)(2,1)S(1)}, u32[]{:S(2)}, u32[]{:S(2)}) async-start(bf16[16,20,128]{2,1,0:T(8,128)(2,1)} %get-tuple-element.14), calls=%async_computation.1 | async-start | bytes 196608 | tf_op jit(solution)/shard_map/all_to_all | solution.py:72
  96.5 4.8 %all-to-all-done.1 = bf16[16,20,128]{2,1,0:T(8,128)(2,1)S(1)} async-done(((bf16[16,20,128]{2,1,0:T(8,128)(2,1)}), bf16[16,20,128]{2,1,0:T(8,128)(2,1)S(1)}, u32[]{:S(2)}, u32[]{:S(2)}) %all-to-all-start.1) | async-done | bytes 81952 | tf_op jit(solution)/shard_map/all_to_all | solution.py:72
  102.1 1.4 fusion.6
  103.5 1.4 fusion.9
  104.9 1.5 fusion.12
  106.5 221.0 %all-reduce.4.cloned.1.call-done = (f32[160,2048]{1,0:T(8,128)}, f32[160,2048]{1,0:T(8,128)}, f32[160,2048]{1,0:T(8,128)}) async-done(((f32[160,2048]{1,0:T(8,128)}, f32[160,2048]{1,0:T(8,128)}, f32[160,2048]{1,0:T(8,128)}), (f32[160,2048]{1,0:T(8,128)}, f32[160,2048]{1,0:T(8,128)}, f32[160,2048]{1,0:T(8,128)})) %all-reduce.4.cloned.1.call-update) | async-done | bytes 3932176 | tf_op jit(solution)/shard_map/psum | solution.py:88
  327.6 3.0 multiply_convert_fusion
  331.0 1.3 fusion.2
  332.3 49.1 %psum.31 = f32[160]{0:T(256)S(1)} all-reduce(f32[160]{0:T(256)S(1)} %fusion.3), channel_id=1, replica_groups=mesh['dp'=32,'expert'=16] {'dp'}, use_global_device_ids=true, to_apply=%region_11.12 | all-reduce | flops 160 | bytes 1280 | tf_op jit(solution)/shard_map/psum | solution.py:98
  381.4 3.4 collective-permute-start
  385.5 1.1 fusion
  386.7 1.0 scatter_custom_fusion.2
  388.3 7.0 %all-to-all-start.2 = ((f32[16,20,128]{2,1,0:T(8,128)}), f32[16,20,128]{2,1,0:T(8,128)S(1)}, u32[]{:S(2)}, u32[]{:S(2)}) async-start(f32[16,20,128]{2,1,0:T(8,128)} %reshape.160), calls=%async_computation.2 | async-start | bytes 393216 | tf_op jit(solution)/shard_map/all_to_all | solution.py:109
  395.3 4.9 %collective-permute-start.1 = (f32[160]{0:T(256)S(1)}, f32[160]{0:T(256)S(1)}, u32[]{:S(2)}, u32[]{:S(2)}) collective-permute-start(f32[160]{0:T(256)S(1)} %add.108), channel_id=1, source_target_pairs={{0,2},{1,3},{2,0},{3,1},{4,6},{5,7},{6,4},{7,5},{8,10},{9,11},{10,... | collective-permute-start | bytes 1928 | tf_op jit(solution)/shard_map/ppermute | solution.py:12
  400.2 1.1 fusion.1
  401.3 1.0 collective-permute-done.1
  402.9 2.0 scatter_custom_fusion.3
  (58 shorter events, 7.8 us)
Async XLA Ops:
  7.2 94.9 %copy-start = (bf16[1,128,2048]{2,1,0:T(8,128)(2,1)S(1)}, bf16[1,128,2048]{2,1,0:T(8,128)(2,1)}, u32[]{:S(2)}) copy-start(bf16[1,128,2048]{2,1,0:T(8,128)(2,1)} %param.11) | copy-start | bytes 1572868
  40.7 30.0 %copy-start.1 = (bf16[320,128]{1,0:T(8,128)(2,1)S(1)}, bf16[320,128]{1,0:T(8,128)(2,1)}, u32[]{:S(2)}) copy-start(bf16[320,128]{1,0:T(8,128)(2,1)} %param.7) | copy-start | bytes 245764
  70.6 1.6 copy-start.2
  74.4 15.6 %all-to-all-start = ((bf16[16,20,128]{2,1,0:T(8,128)(2,1)}), bf16[16,20,128]{2,1,0:T(8,128)(2,1)S(1)}, u32[]{:S(2)}, u32[]{:S(2)}) async-start(bf16[16,20,128]{2,1,0:T(8,128)(2,1)} %get-tuple-element.13), calls=%async_computation | async-start | bytes 196608 | tf_op jit(solution)/shard_map/all_to_all | solution.py:73
  90.0 11.3 %all-to-all-start.1 = ((bf16[16,20,128]{2,1,0:T(8,128)(2,1)}), bf16[16,20,128]{2,1,0:T(8,128)(2,1)S(1)}, u32[]{:S(2)}, u32[]{:S(2)}) async-start(bf16[16,20,128]{2,1,0:T(8,128)(2,1)} %get-tuple-element.14), calls=%async_computation.1 | async-start | bytes 196608 | tf_op jit(solution)/shard_map/all_to_all | solution.py:72
  95.0 232.6 %all-reduce.4.cloned.1.call-start = ((), (), s32[]{:S(2)}) async-start(), calls=%async_computation.3 | async-start | bytes 7864320 | tf_op jit(solution)/shard_map/psum | solution.py:88
  95.7 7.8 %copy-start.4 = (bf16[1,128,2048]{2,1,0:T(8,128)(2,1)S(1)}, bf16[1,128,2048]{2,1,0:T(8,128)(2,1)}, u32[]{:S(2)}) copy-start(bf16[1,128,2048]{2,1,0:T(8,128)(2,1)} %param.12) | copy-start | bytes 1572868
  103.5 1.4 copy-start.3
  381.4 13.9 %collective-permute-start = (f32[160]{0:T(256)S(1)}, f32[160]{0:T(256)S(1)}, u32[]{:S(2)}, u32[]{:S(2)}) collective-permute-start(f32[160]{0:T(256)S(1)} %psum.31), channel_id=1, source_target_pairs={{0,1},{1,0},{2,3},{3,2},{4,5},{5,4},{6,7},{7,6},{8,9},{9,8},{10,11... | collective-permute-start | bytes 1928 | tf_op jit(solution)/shard_map/ppermute | solution.py:12
  388.3 14.6 %all-to-all-start.2 = ((f32[16,20,128]{2,1,0:T(8,128)}), f32[16,20,128]{2,1,0:T(8,128)S(1)}, u32[]{:S(2)}, u32[]{:S(2)}) async-start(f32[16,20,128]{2,1,0:T(8,128)} %reshape.160), calls=%async_computation.2 | async-start | bytes 393216 | tf_op jit(solution)/shard_map/all_to_all | solution.py:109
  395.3 7.0 %collective-permute-start.1 = (f32[160]{0:T(256)S(1)}, f32[160]{0:T(256)S(1)}, u32[]{:S(2)}, u32[]{:S(2)}) collective-permute-start(f32[160]{0:T(256)S(1)} %add.108), channel_id=1, source_target_pairs={{0,2},{1,3},{2,0},{3,1},{4,6},{5,7},{6,4},{7,5},{8,10},{9,11},{10,... | collective-permute-start | bytes 1928 | tf_op jit(solution)/shard_map/ppermute | solution.py:12
Sparse Core Ops, SparseCore 0:
  106.5 221.0 all-reduce.3
where the time goes:
time: 413 us; the launch traced here: 412 us
  waiting for transfers between devices  233 us (56%)
  local copies, waits for them, and re-layouts  68.4 us (17%)
  blocking collectives  49.1 us (12%)
  starting transfers between devices  29.4 us (7%)
  between operations  14.3 us (3%)
  other arithmetic  9.07 us (2%)
  matrix products  8.98 us (2%)
    psum x1, waiting for transfers between devices, per_device(): pre_gate, pre_up = lax.psum((part_gate, part_up), 'dp')  221 us
    psum x1, blocking collectives, per_device(): gate_total = lax.psum(gate_part, 'dp')  49.1 us
    scatter x1, local copies, waits for them, and re-layouts, per_device(): send_table = jnp.zeros((flight_count, bucket_size + 1), jnp.int32).at[exp...  29.9 us
    scatter x1, local copies, waits for them, and re-layouts, per_device(): filled = jnp.zeros((flight_count, bucket_size + 1), jnp.int32).at[expert_...  29.9 us
    all_to_all x1, starting transfers between devices, per_device(): lax.all_to_all(grad_send, 'expert', split_axis=0, concat_axis=0, tiled=True)  9.2 us
    ppermute x2, starting transfers between devices, partner(): return lax.ppermute(value, axis, pairs)  8.27 us
  transfers between devices with their start and end apart: 6, of which 4 were waited for; matrix products, arithmetic and copies ran while one was open for 2% of the time, Pallas kernels for 0%

commit v1 on v0

--- a/solution.py
+++ b/solution.py
@@ -95,7 +95,8 @@
     part_hidden = contract_cols(scaled, down_weight)
     grad_hidden = lax.psum(part_hidden, "dp")
     gate_side, up_side = gated_grads(grad_hidden, pre_gate, pre_up, sigmoid_gate)
-    gate_total = lax.psum(gate_part, "dp")
+    parts = lax.all_gather(gate_part, "dp", axis=0, tiled=False)
+    gate_total = parts.sum(axis=0)
     grad_gate_weight = contract_rows(slot_inputs, gate_side).astype(jnp.bfloat16)
     grad_up_weight = contract_rows(slot_inputs, up_side).astype(jnp.bfloat16)
     slot_back = contract_cols(gate_side, gate_weight) + contract_cols(up_side, up_weight)

time: 413 us -> 458 us (1.11)
  blocking collectives: 49.1 us -> 93.3 us
    unnamed x0 -> x1, blocking collectives: none -> 93.3 us
    psum x1 -> x0, blocking collectives: 49.1 us -> none  [per_device(): gate_total = lax.psum(gate_part, 'dp')]
where the time goes in v1:
time: 458 us; the launch traced here: 457 us
  waiting for transfers between devices  231 us (50%)
  blocking collectives  93.3 us (20%)
  local copies, waits for them, and re-layouts  70 us (15%)
  starting transfers between devices  29.4 us (6%)
  between operations  15 us (3%)
  other arithmetic  9.13 us (2%)
  matrix products  8.95 us (2%)
    psum x1, waiting for transfers between devices, per_device(): pre_gate, pre_up = lax.psum((part_gate, part_up), 'dp')  219 us
    unnamed x1, blocking collectives  93.3 us
    scatter x1, local copies, waits for them, and re-layouts, per_device(): filled = jnp.zeros((flight_count, bucket_size + 1), jnp.int32).at[expert_...  29.9 us
    scatter x1, local copies, waits for them, and re-layouts, per_device(): send_table = jnp.zeros((flight_count, bucket_size + 1), jnp.int32).at[exp...  29.9 us
    all_to_all x1, starting transfers between devices, per_device(): lax.all_to_all(input_send, 'expert', split_axis=0, concat_axis=0, tiled=T...  9.2 us
  transfers between devices with their start and end apart: 6, of which 4 were waited for; matrix products, arithmetic and copies ran while one was open for 2% of the time, Pallas kernels for 0%

profile of v1, /device:TPU:2, one launch (start us, length us, event | category | flops | bytes accessed | tf_op | source)
XLA Modules:
  0.0 457.1 jit_solution(13081997900001145920)
XLA Ops:
  8.0 2.3 reduce-window.6
  10.8 29.9 %scatter_fusion = s32[4,21]{1,0:T(4,128)S(1)} fusion(s32[4,21]{1,0:T(4,128)S(1)} %broadcast.144.clone.1, s32[640]{0:T(1024)S(1)} %reshape.195, s32[640]{0:T(1024)S(1)} %broadcast.189), kind=kCustom, calls=%fused_computation.4 | custom fusion | bytes 12800 | tf_op jit(solution)/shard_map/scatter | solution.py:65
  40.7 29.9 %scatter_fusion.1 = s32[4,21]{1,0:T(4,128)S(1)} fusion(s32[4,21]{1,0:T(4,128)S(1)} %broadcast.144.clone, s32[640]{0:T(1024)S(1)} %reshape.195, s32[640]{0:T(1024)S(1)} %reshape.203), kind=kCustom, calls=%fused_computation.5 | custom fusion | bytes 12800 | tf_op jit(solution)/shard_map/scatter | solution.py:60
  70.7 1.4 gather_fusion
  72.2 1.4 gather_fusion.2
  74.4 9.2 %all-to-all-start.1 = ((bf16[16,20,128]{2,1,0:T(8,128)(2,1)}), bf16[16,20,128]{2,1,0:T(8,128)(2,1)S(1)}, u32[]{:S(2)}, u32[]{:S(2)}) async-start(bf16[16,20,128]{2,1,0:T(8,128)(2,1)} %get-tuple-element.14), calls=%async_computation.1 | async-start | bytes 196608 | tf_op jit(solution)/shard_map/all_to_all | solution.py:72
  83.7 6.4 %all-to-all-done.1 = bf16[16,20,128]{2,1,0:T(8,128)(2,1)S(1)} async-done(((bf16[16,20,128]{2,1,0:T(8,128)(2,1)}), bf16[16,20,128]{2,1,0:T(8,128)(2,1)S(1)}, u32[]{:S(2)}, u32[]{:S(2)}) %all-to-all-start.1) | async-done | bytes 81952 | tf_op jit(solution)/shard_map/all_to_all | solution.py:72
  90.0 5.0 %all-to-all-start = ((bf16[16,20,128]{2,1,0:T(8,128)(2,1)}), bf16[16,20,128]{2,1,0:T(8,128)(2,1)S(1)}, u32[]{:S(2)}, u32[]{:S(2)}) async-start(bf16[16,20,128]{2,1,0:T(8,128)(2,1)} %get-tuple-element.13), calls=%async_computation | async-start | bytes 196608 | tf_op jit(solution)/shard_map/all_to_all | solution.py:73
  96.5 4.8 %all-to-all-done = bf16[16,20,128]{2,1,0:T(8,128)(2,1)S(1)} async-done(((bf16[16,20,128]{2,1,0:T(8,128)(2,1)}), bf16[16,20,128]{2,1,0:T(8,128)(2,1)S(1)}, u32[]{:S(2)}, u32[]{:S(2)}) %all-to-all-start) | async-done | bytes 81952 | tf_op jit(solution)/shard_map/all_to_all | solution.py:73
  102.1 1.4 fusion.6
  103.5 1.4 fusion.9
  104.9 1.5 fusion.12
  106.5 1.3 dynamic-slice
  108.5 219.1 %all-reduce.5.cloned.1.call-done = (f32[160,2048]{1,0:T(8,128)}, f32[160,2048]{1,0:T(8,128)}, f32[160,2048]{1,0:T(8,128)}) async-done(((f32[160,2048]{1,0:T(8,128)}, f32[160,2048]{1,0:T(8,128)}, f32[160,2048]{1,0:T(8,128)}), (f32[160,2048]{1,0:T(8,128)}, f32[160,2048]{1,0:T(8,128)}, f32[160,2048]{1,0:T(8,128)})) %all-reduce.5.cloned.1.call-update) | async-done | bytes 3932176 | tf_op jit(solution)/shard_map/psum | solution.py:88
  327.6 3.0 multiply_convert_fusion
  330.6 1.3 fusion.2
  333.1 93.3 %all-reduce.1 = f32[5120]{0:T(1024)S(1)} all-reduce(f32[5120]{0:T(1024)S(1)} %dynamic-update-slice), channel_id=2, replica_groups=mesh['dp'=32,'expert'=16] {'dp'}, use_global_device_ids=true, to_apply=%add.1 | all-reduce | flops 5120 | bytes 40960
  426.4 3.4 collective-permute-start
  430.2 1.1 fusion
  433.0 7.0 %all-to-all-start.2 = ((f32[16,20,128]{2,1,0:T(8,128)}), f32[16,20,128]{2,1,0:T(8,128)S(1)}, u32[]{:S(2)}, u32[]{:S(2)}) async-start(f32[16,20,128]{2,1,0:T(8,128)} %reshape.160), calls=%async_computation.2 | async-start | bytes 393216 | tf_op jit(solution)/shard_map/all_to_all | solution.py:110
  440.0 4.9 %collective-permute-start.1 = (f32[160]{0:T(256)S(1)}, f32[160]{0:T(256)S(1)}, u32[]{:S(2)}, u32[]{:S(2)}) collective-permute-start(f32[160]{0:T(256)S(1)} %add.106), channel_id=1, source_target_pairs={{0,2},{1,3},{2,0},{3,1},{4,6},{5,7},{6,4},{7,5},{8,10},{9,11},{10,... | collective-permute-start | bytes 1928 | tf_op jit(solution)/shard_map/ppermute | solution.py:12
  444.9 1.1 fusion.1
  446.0 1.0 collective-permute-done.1
  447.6 2.0 scatter_custom_fusion.3
  (63 shorter events, 9.2 us)
Async XLA Ops:
  7.2 94.9 %copy-start = (bf16[1,128,2048]{2,1,0:T(8,128)(2,1)S(1)}, bf16[1,128,2048]{2,1,0:T(8,128)(2,1)}, u32[]{:S(2)}) copy-start(bf16[1,128,2048]{2,1,0:T(8,128)(2,1)} %param.11) | copy-start | bytes 1572868
  40.7 30.0 %copy-start.1 = (bf16[320,128]{1,0:T(8,128)(2,1)S(1)}, bf16[320,128]{1,0:T(8,128)(2,1)}, u32[]{:S(2)}) copy-start(bf16[320,128]{1,0:T(8,128)(2,1)} %param.8) | copy-start | bytes 245764
  70.6 1.6 copy-start.2
  74.4 15.6 %all-to-all-start.1 = ((bf16[16,20,128]{2,1,0:T(8,128)(2,1)}), bf16[16,20,128]{2,1,0:T(8,128)(2,1)S(1)}, u32[]{:S(2)}, u32[]{:S(2)}) async-start(bf16[16,20,128]{2,1,0:T(8,128)(2,1)} %get-tuple-element.14), calls=%async_computation.1 | async-start | bytes 196608 | tf_op jit(solution)/shard_map/all_to_all | solution.py:72
  90.0 11.3 %all-to-all-start = ((bf16[16,20,128]{2,1,0:T(8,128)(2,1)}), bf16[16,20,128]{2,1,0:T(8,128)(2,1)S(1)}, u32[]{:S(2)}, u32[]{:S(2)}) async-start(bf16[16,20,128]{2,1,0:T(8,128)(2,1)} %get-tuple-element.13), calls=%async_computation | async-start | bytes 196608 | tf_op jit(solution)/shard_map/all_to_all | solution.py:73
  95.0 232.6 %all-reduce.5.cloned.1.call-start = ((), (), s32[]{:S(2)}) async-start(), calls=%async_computation.3 | async-start | bytes 7864320 | tf_op jit(solution)/shard_map/psum | solution.py:88
  95.8 7.8 %copy-start.4 = (bf16[1,128,2048]{2,1,0:T(8,128)(2,1)S(1)}, bf16[1,128,2048]{2,1,0:T(8,128)(2,1)}, u32[]{:S(2)}) copy-start(bf16[1,128,2048]{2,1,0:T(8,128)(2,1)} %param.12) | copy-start | bytes 1572868
  103.5 1.4 copy-start.3
  426.4 13.5 %collective-permute-start = (f32[160]{0:T(256)S(1)}, f32[160]{0:T(256)S(1)}, u32[]{:S(2)}, u32[]{:S(2)}) collective-permute-start(f32[160]{0:T(256)S(1)} %reduce_sum.29), channel_id=1, source_target_pairs={{0,1},{1,0},{2,3},{3,2},{4,5},{5,4},{6,7},{7,6},{8,9},{9,8},{10,11... | collective-permute-start | bytes 1928 | tf_op jit(solution)/shard_map/ppermute | solution.py:12
  433.0 14.6 %all-to-all-start.2 = ((f32[16,20,128]{2,1,0:T(8,128)}), f32[16,20,128]{2,1,0:T(8,128)S(1)}, u32[]{:S(2)}, u32[]{:S(2)}) async-start(f32[16,20,128]{2,1,0:T(8,128)} %reshape.160), calls=%async_computation.2 | async-start | bytes 393216 | tf_op jit(solution)/shard_map/all_to_all | solution.py:110
  440.0 7.0 %collective-permute-start.1 = (f32[160]{0:T(256)S(1)}, f32[160]{0:T(256)S(1)}, u32[]{:S(2)}, u32[]{:S(2)}) collective-permute-start(f32[160]{0:T(256)S(1)} %add.106), channel_id=1, source_target_pairs={{0,2},{1,3},{2,0},{3,1},{4,6},{5,7},{6,4},{7,5},{8,10},{9,11},{10,... | collective-permute-start | bytes 1928 | tf_op jit(solution)/shard_map/ppermute | solution.py:12
Sparse Core Ops, SparseCore 0:
  106.5 221.0 all-reduce.4
